TPU v7x, 256 devices: a whole 4x4x8 slice. The times are simulated.
256 devices in a mesh: member: 16 (over y, x_hi, core), dp: 16 (over z, x_lo).
Axes of the slice: x: 4 (x_hi: 2, x_lo: 2; x = x_hi * 2 + x_lo), y: 4, z: 8, core: 2. Of those that a mesh axis runs over, the one named last changes fastest.
Arguments:
- teacher_tokens: bfloat16 [2752, 1536], P('dp'), may hold values from -100 to 100
- teacher_qkv: bfloat16 [16, 1536, 4608], P('member', None, 'dp'), may hold values from -0.15625 to 0.15625
- student_tokens: bfloat16 [2752, 1024], P('dp'), may hold values from -6 to 6
- student_gain: float32 [1024], replicated, may hold values from 0.1 to 1.9
- w_up: bfloat16 [1024, 4096], P(None, 'member'), may hold values from -0.1875 to 0.1875
- w_down: bfloat16 [1024, 4096], P(None, 'member'), may hold values from -0.09375 to 0.09375
- w_head: bfloat16 [1024, 1536], P(None, 'member'), may hold values from -0.1875 to 0.1875
Outputs:
- grad_up: float32 [1024, 4096], P('dp', 'member')
- grad_down: float32 [1024, 4096], P('dp', 'member')
- grad_head: float32 [1024, 1536], P('dp', 'member')
All inputs are finite; a program needn't handle non-finite values.
Results may differ from a plain program's by a relative error of at most 0.0055.
Values may be sent and summed in bfloat16 or wider, within the bound.
No kernel may reach another device: no remote copies, remote signals or barrier semaphores. Data moves between devices by JAX's collectives and lax.ppermute only.
A program may use at most 192 MiB of HBM per device.

v0:
```python
from functools import partial
import math
import jax
import jax.numpy as jnp
from jax import lax
from jax.sharding import PartitionSpec as P

VALID = 1370
IMAGES = 2


def body(teacher_tokens, teacher_qkv, student_tokens, student_gain, w_up, w_down, w_head):
    tok_rows = teacher_tokens.shape[0]
    feat_width = teacher_tokens.shape[1]
    head_count = feat_width // 64
    own_columns = teacher_qkv[0]
    query_slots = lax.axis_index("dp") * tok_rows + jnp.arange(tok_rows, dtype=jnp.int32)
    query_image = query_slots % IMAGES
    real_query = query_slots // IMAGES < VALID
    projected = jnp.dot(
        teacher_tokens,
        lax.all_gather(own_columns, "dp", axis=1, tiled=True),
        preferred_element_type=jnp.float32,
    ).astype(jnp.bfloat16)
    queries = projected[:, :feat_width].reshape(tok_rows, head_count, 64)
    keys_local = projected[:, feat_width : 2 * feat_width]
    values_local = projected[:, 2 * feat_width :]
    row_max = jnp.full((head_count, tok_rows), -1e30, jnp.float32)
    weighted = jnp.zeros((tok_rows, head_count, 64), jnp.float32)
    key_heads = lax.all_gather(keys_local, "dp", axis=0, tiled=True).reshape(-1, head_count, 64)
    value_heads = lax.all_gather(values_local, "dp", axis=0, tiled=True).reshape(-1, head_count, 64)
    key_slots = jnp.arange(key_heads.shape[0], dtype=jnp.int32)
    allowed = (query_image[:, None] == (key_slots % IMAGES)[None, :]) & (
        key_slots // IMAGES < VALID
    )[None, :]
    scores = (
        jnp.einsum("qhd,khd->hqk", queries, key_heads, preferred_element_type=jnp.float32) * 0.125
    )
    scores = jnp.where(allowed[None], scores, -1e30)
    new_max = jnp.maximum(row_max, jnp.max(scores, axis=-1))
    factor = jnp.exp(row_max - new_max)
    expsc = jnp.where(allowed[None], jnp.exp(scores - new_max[:, :, None]), 0.0)
    denom_sum = jnp.sum(expsc, axis=-1)
    update = jnp.einsum(
        "hqk,khd->qhd", expsc.astype(jnp.bfloat16), value_heads, preferred_element_type=jnp.float32
    )
    weighted = weighted * factor.T[:, :, None] + update
    row_max, denom_sum, weighted = (new_max, denom_sum, weighted)
    context = (weighted / denom_sum.T[:, :, None]).reshape(tok_rows, feat_width)
    member_slot = lax.axis_index("member")
    share_width = feat_width // lax.axis_size("member")
    summed = lax.psum(context, "member")
    row_mean = jnp.mean(summed, axis=-1, keepdims=True)
    mean_square = jnp.mean(summed * summed, axis=-1, keepdims=True)
    full_target = (summed - row_mean) * lax.rsqrt(mean_square - row_mean * row_mean + 1e-06)
    target = lax.dynamic_slice_in_dim(full_target, member_slot * share_width, share_width, 1)
    inputs = student_tokens.astype(jnp.float32)
    in_mean = jnp.mean(inputs, axis=-1, keepdims=True)
    in_var = jnp.mean((inputs - in_mean) ** 2, axis=-1, keepdims=True)
    normed = ((inputs - in_mean) * lax.rsqrt(in_var + 1e-06) * student_gain).astype(jnp.bfloat16)
    pre = jnp.dot(normed, w_up, preferred_element_type=jnp.float32)
    gelu_tanh = partial(jax.nn.gelu, approximate=True)
    hidden = gelu_tanh(pre).astype(jnp.bfloat16)
    branch_part = lax.dot_general(
        hidden, w_down, (((1,), (1,)), ((), ())), preferred_element_type=jnp.float32
    )
    student_out = (inputs + lax.psum(branch_part, "member")).astype(jnp.bfloat16)
    pred = jnp.dot(student_out, w_head, preferred_element_type=jnp.float32)
    pred_grad = jnp.where(
        real_query[:, None], (pred - target) / math.sqrt(IMAGES * VALID), 0.0
    ).astype(jnp.bfloat16)
    grad_head = lax.dot_general(
        student_out, pred_grad, (((0,), (0,)), ((), ())), preferred_element_type=jnp.float32
    )
    out_part = lax.dot_general(
        pred_grad, w_head, (((1,), (1,)), ((), ())), preferred_element_type=jnp.float32
    )
    out_grad = lax.psum(out_part, "member").astype(jnp.bfloat16)
    grad_down = lax.dot_general(
        out_grad, hidden, (((0,), (0,)), ((), ())), preferred_element_type=jnp.float32
    )
    hidden_grad = jnp.dot(out_grad, w_down, preferred_element_type=jnp.float32)
    _, pullback = jax.vjp(gelu_tanh, pre)
    pre_grad = pullback(hidden_grad)[0].astype(jnp.bfloat16)
    grad_up = lax.dot_general(
        normed, pre_grad, (((0,), (0,)), ((), ())), preferred_element_type=jnp.float32
    )
    grad_up, grad_down, grad_head = (
        lax.psum_scatter(grad_up, "dp", scatter_dimension=0, tiled=True),
        lax.psum_scatter(grad_down, "dp", scatter_dimension=0, tiled=True),
        lax.psum_scatter(grad_head, "dp", scatter_dimension=0, tiled=True),
    )
    return (grad_up, grad_down, grad_head)


def solution(mesh):
    in_specs = (
        P("dp", None),
        P("member", None, "dp"),
        P("dp", None),
        P(),
        P(None, "member"),
        P(None, "member"),
        P(None, "member"),
    )
    out_specs = (P("dp", "member"), P("dp", "member"), P("dp", "member"))
    return jax.shard_map(body, mesh=mesh, in_specs=in_specs, out_specs=out_specs, check_vma=False)
```

profile of v0, /device:TPU:8, one launch (start us, length us, event | category | flops | bytes accessed | tf_op | source)
XLA Modules:
  0.0 1197.4 jit_solution(361960012682249767)
XLA Ops:
  7.3 0.7 all-gather.7.cloned.1.call-update
  8.0 303.0 %all-gather.7.cloned.1.call-done = bf16[1,1536,4608]{1,2,0:T(8,128)(2,1)} async-done(((bf16[1,1536,288]{1,2,0:T(8,128)(2,1)}), bf16[1,1536,4608]{1,2,0:T(8,128)(2,1)}) %all-gather.7.cloned.1.call-update) | async-done | bytes 14155792 | tf_op jit(solution)/shard_map/all_gather | solution.py:22
  311.0 9.7 fusion.8
  320.7 1.2 slice_bitcast_fusion.1
  322.0 0.7 all-gather.9.cloned.1.call-update
  322.8 0.1 convert_reduce_fusion
  322.9 0.2 fusion.19
  323.2 0.3 fusion.71
  323.5 1.2 fusion.69
  324.7 0.4 compare_and_fusion
  325.1 0.3 copy.18
  325.4 186.0 %all-gather.11.cloned.1.call-done = bf16[16,172,1536]{2,1,0:T(8,128)(2,1)} async-done(((bf16[1,172,1536]{2,1,0:T(8,128)(2,1)}), bf16[16,172,1536]{2,1,0:T(8,128)(2,1)}) %all-gather.11.cloned.1.call-update) | async-done | bytes 8454160 | tf_op jit(solution)/shard_map/all_gather | solution.py:31
  511.4 17.4 %copy.20 = bf16[16,172,1536]{1,0,2:T(8,128)(2,1)} copy(bf16[16,172,1536]{2,1,0:T(8,128)(2,1)} %all-gather.11.cloned.1.call-done) | data formatting | bytes 16908288 | tf_op jit(solution)/shard_map/all_gather | solution.py:31
  528.8 22.6 %reshape.154 = bf16[2752,24,64]{0,2,1:T(8,128)(2,1)} reshape(bf16[16,172,1536]{1,0,2:T(8,128)(2,1)} %copy.20) | data formatting | bytes 16908288 | tf_op jit(solution)/shard_map/reshape | solution.py:31
  551.4 150.4 %all-gather.9.cloned.1.call-done = bf16[16,172,1536]{2,1,0:T(8,128)(2,1)} async-done(((bf16[1,172,1536]{2,1,0:T(8,128)(2,1)}), bf16[16,172,1536]{2,1,0:T(8,128)(2,1)}) %all-gather.9.cloned.1.call-update) | async-done | bytes 8454160 | tf_op jit(solution)/shard_map/all_gather | solution.py:30
  701.8 17.4 %copy.19 = bf16[16,172,1536]{1,0,2:T(8,128)(2,1)} copy(bf16[16,172,1536]{2,1,0:T(8,128)(2,1)} %all-gather.9.cloned.1.call-done) | data formatting | bytes 16908288 | tf_op jit(solution)/shard_map/all_gather | solution.py:30
  719.2 22.6 %reshape.153 = bf16[2752,24,64]{0,2,1:T(8,128)(2,1)} reshape(bf16[16,172,1536]{1,0,2:T(8,128)(2,1)} %copy.19) | data formatting | bytes 16908288 | tf_op jit(solution)/shard_map/reshape | solution.py:30
  741.8 21.7 %fusion = (f32[24,172]{1,0:T(8,128)S(1)}, f32[24,172,2752]{2,1,0:T(8,128)}) fusion(pred[172,2752]{1,0:T(8,128)(4,1)S(1)} %compare_and_fusion, bf16[172,24,64]{0,2,1:T(8,128)(2,1)S(1)} %bitcast.35, bf16[2752,24,64]{0,2,1:T(8,128)(2,1)} %reshape.153), kind=kOutput, calls=%fused_computation.2 | convolution fusion | flops 1488189440 | bytes 54913408 | tf_op jit(solution)/shard_map/qhd,khd->hqk/dot_general | solution.py:37
  763.5 22.9 %fusion.1 = f32[24,172]{1,0:T(8,128)S(1)} fusion(f32[24,172,2752]{2,1,0:T(8,128)} %get-tuple-element.15, f32[24,172]{1,0:T(8,128)S(1)} %get-tuple-element.11, pred[172,2752]{1,0:T(8,128)(4,1)S(1)} %compare_and_fusion), kind=kLoop, calls=%fused_computation.3 | loop fusion | flops 56797152 | bytes 45947392 | tf_op jit(solution)/shard_map/reduce_sum | solution.py:43
  786.4 20.8 %fusion.11 = f32[172,24,64]{0,2,1:T(8,128)S(1)} fusion(bf16[2752,24,64]{0,2,1:T(8,128)(2,1)} %reshape.154, f32[24,172,2752]{2,1,0:T(8,128)} %get-tuple-element.15, f32[24,172]{1,0:T(8,128)S(1)} %get-tuple-element.11, pred[172,2752]{1,0:T(8,128)(4,1)S(1)} %compare_and_fusion, f32[172,24]{0,1:T(8,128)S(1)} %bitcast.37, f32[172,24]{0,1:T(8,128)S(1)} %get-tuple-element.10), kind=kOutput, calls=%fused_computation.12 | convolution fusion | flops 1511442432 | bytes 55474816 | tf_op jit(solution)/shard_map/hqk,khd->qhd/dot_general | solution.py:44
  807.3 1.5 copy.21
  808.8 144.0 %all-reduce.4.cloned.1.call-done = (f32[172,1536]{1,0:T(8,128)}, f32[172,1024]{1,0:T(8,128)}) async-done(((f32[172,1536]{1,0:T(8,128)}, f32[172,1024]{1,0:T(8,128)}), (f32[172,1536]{1,0:T(8,128)}, f32[172,1024]{1,0:T(8,128)})) %all-reduce.4.cloned.1.call-update) | async-done | bytes 1761296 | tf_op jit(solution)/shard_map/psum | solution.py:52
  952.9 1.5 fusion.73
  954.3 1.4 fusion.16
  955.8 0.2 fusion.74
  956.0 2.3 fusion.66
  958.3 0.0 reduce-scatter.4.cloned.1.call-start
  958.4 77.2 %all-reduce.5 = bf16[172,1024]{1,0:T(8,128)(2,1)S(1)} all-reduce(f32[172,1024]{1,0:T(8,128)S(1)} %fusion.74), channel_id=1, replica_groups=mesh['member'=16,'dp'=16] {'member'}, use_global_device_ids=true, to_apply=%region_8.9 | all-reduce | flops 176128 | bytes 1056768 | tf_op jit(solution)/shard_map/psum | solution.py:78
  1035.6 2.8 fusion.37
  1038.4 1.4 fusion.30
  1039.8 76.7 %reduce-scatter.4.cloned.1.call-done = f32[64,256]{1,0:T(8,128)} async-done(((f32[1024,256]{1,0:T(8,128)}), f32[64,256]{1,0:T(8,128)}) %reduce-scatter.4.cloned.1.call-update) | async-done | bytes 65552 | tf_op jit(solution)/shard_map/reduce_scatter | solution.py:89
  1116.6 74.0 %reduce-scatter.6.cloned.1.call-done = f32[64,256]{1,0:T(8,128)} async-done(((f32[1024,256]{1,0:T(8,128)}), f32[64,256]{1,0:T(8,128)}) %reduce-scatter.6.cloned.1.call-update) | async-done | bytes 65552 | tf_op jit(solution)/shard_map/reduce_scatter | solution.py:90
  (34 shorter events, 0.5 us)
Async XLA Ops:
  7.2 303.8 %copy-start = (bf16[172,1536]{1,0:T(8,128)(2,1)S(1)}, bf16[172,1536]{1,0:T(8,128)(2,1)}, u32[]{:S(2)}) copy-start(bf16[172,1536]{1,0:T(8,128)(2,1)} %param.7) | copy-start | bytes 1585156
  7.2 315.6 %copy-start.2 = (bf16[172,1024]{1,0:T(8,128)(2,1)S(1)}, bf16[172,1024]{1,0:T(8,128)(2,1)}, u32[]{:S(2)}) copy-start(bf16[172,1024]{1,0:T(8,128)(2,1)} %param.9) | copy-start | bytes 1056772
  7.2 316.0 %copy-start.5 = (bf16[1024,256]{1,0:T(8,128)(2,1)S(1)}, bf16[1024,256]{1,0:T(8,128)(2,1)}, u32[]{:S(2)}) copy-start(bf16[1024,256]{1,0:T(8,128)(2,1)} %param.11) | copy-start | bytes 1572868
  7.2 316.0 %copy-start.6 = (f32[1024]{0:T(1024)S(1)}, f32[1024]{0:T(1024)}, u32[]{:S(2)}) copy-start(f32[1024]{0:T(1024)} %param.10) | copy-start | bytes 12292
  7.2 316.3 %copy-start.4 = (bf16[1024,256]{1,0:T(8,128)(2,1)S(1)}, bf16[1024,256]{1,0:T(8,128)(2,1)}, u32[]{:S(2)}) copy-start(bf16[1024,256]{1,0:T(8,128)(2,1)} %param.12) | copy-start | bytes 1572868
  7.2 303.8 %all-gather.7.cloned.1.call-start = ((), (), s32[]{:S(2)}) async-start(), calls=%async_computation.6 | async-start | bytes 15040512 | tf_op jit(solution)/shard_map/all_gather | solution.py:22
  8.0 503.5 %all-gather.11.cloned.1.call-start = ((), (), s32[]{:S(2)}) async-start(), calls=%async_computation.8 | async-start | bytes 9191424 | tf_op jit(solution)/shard_map/all_gather | solution.py:31
  321.9 379.9 %all-gather.9.cloned.1.call-start = ((), (), s32[]{:S(2)}) async-start(), calls=%async_computation.7 | async-start | bytes 9191424 | tf_op jit(solution)/shard_map/all_gather | solution.py:30
  322.7 630.2 %all-reduce.4.cloned.1.call-start = ((), (), s32[]{:S(2)}) async-start(), calls=%async_computation.9 | async-start | bytes 3604480 | tf_op jit(solution)/shard_map/psum | solution.py:52
  786.4 167.9 %copy-start.3 = (bf16[1024,96]{0,1:T(8,128)(2,1)S(1)}, bf16[1024,96]{0,1:T(8,128)(2,1)}, u32[]{:S(2)}) copy-start(bf16[1024,96]{0,1:T(8,128)(2,1)} %param.13) | copy-start | bytes 589828
  786.4 404.2 %copy-start.1 = (bf16[172,1536]{1,0:T(8,128)(2,1)S(1)}, bf16[172,1536]{1,0:T(8,128)(2,1)}, u32[]{:S(2)}) copy-start(bf16[172,1536]{1,0:T(8,128)(2,1)} %param.7) | copy-start | bytes 1585156
  808.8 231.1 %reduce-scatter.8.cloned.1.call-start = ((), (), s32[]{:S(2)}) async-start(), calls=%async_computation.5 | async-start | bytes 557056 | tf_op jit(solution)/shard_map/reduce_scatter | solution.py:91
  958.3 158.2 %reduce-scatter.4.cloned.1.call-start = ((), (), s32[]{:S(2)}) async-start(), calls=%async_computation.3 | async-start | bytes 1114112 | tf_op jit(solution)/shard_map/reduce_scatter | solution.py:89
  1038.4 152.2 %reduce-scatter.6.cloned.1.call-start = ((), (), s32[]{:S(2)}) async-start(), calls=%async_computation.4 | async-start | bytes 1114112 | tf_op jit(solution)/shard_map/reduce_scatter | solution.py:90
Sparse Core Ops, SparseCore 0:
  9.8 301.1 all-gather.6
  322.0 189.3 all-gather.10
  513.2 188.5 all-gather.8
  808.9 143.9 all-reduce.3
  958.4 79.0 reduce-scatter.7
  1040.5 75.9 reduce-scatter.3
  1119.6 70.9 reduce-scatter.5
where the time goes:
time: 1200 us
  waiting for transfers between devices  936 us (78%)
  local copies, waits for them, and re-layouts  83 us (7%)
  blocking collectives  77.2 us (6%)
  matrix products  61.8 us (5%)
  other arithmetic  25.2 us (2%)
  between operations  14.3 us (1%)
    all_gather x1, waiting for transfers between devices, body(): lax.all_gather(own_columns, 'dp', axis=1, tiled=True)  303 us
    all_gather x1, waiting for transfers between devices, body(): lax.all_gather(values_local, 'dp', axis=0, tiled=True)  186 us
    all_gather x1, waiting for transfers between devices, body(): lax.all_gather(keys_local, 'dp', axis=0, tiled=True)  150 us
    psum x1, waiting for transfers between devices, body(): summed = lax.psum(context, 'member')  144 us
    psum x1, blocking collectives, body(): out_grad = lax.psum(out_part, 'member').astype(jnp.bfloat16)  77.2 us
    reduce_scatter x1, waiting for transfers between devices, body(): lax.psum_scatter(grad_up, 'dp', scatter_dimension=0, tiled=True)  76.7 us
    reduce_scatter x1, waiting for transfers between devices, body(): lax.psum_scatter(grad_down, 'dp', scatter_dimension=0, tiled=True)  74 us
  transfers between devices with their start and end apart: 7, of which 6 were waited for; matrix products, arithmetic and copies ran while one was open for 4% of the time, Pallas kernels for 0%

commit v1 on v0

--- a/solution.py
+++ b/solution.py
@@ -49,7 +49,7 @@
     context = (weighted / denom_sum.T[:, :, None]).reshape(tok_rows, feat_width)
     member_slot = lax.axis_index("member")
     share_width = feat_width // lax.axis_size("member")
-    summed = lax.psum(context, "member")
+    summed = jnp.sum(lax.all_gather(context, "member"), axis=0)
     row_mean = jnp.mean(summed, axis=-1, keepdims=True)
     mean_square = jnp.mean(summed * summed, axis=-1, keepdims=True)
     full_target = (summed - row_mean) * lax.rsqrt(mean_square - row_mean * row_mean + 1e-06)

time: 1200 us -> 1310 us (1.092)
  waiting for transfers between devices: 936 us -> 1030 us
    all_gather x0 -> x1, waiting for transfers between devices: none -> 111 us  [body(): summed = jnp.sum(lax.all_gather(context, 'member'), axis=0)]
    psum x1, waiting for transfers between devices: 144 us -> 129 us  [body(): lax.psum(branch_part, 'member')]
  transfers between devices with their start and end apart: 7 -> 8, of which waited for: 6 -> 7; matrix products, arithmetic and copies ran while one was open for 4% -> 5% of each run, Pallas kernels for 0% -> 0%
where the time goes in v1:
time: 1310 us
  waiting for transfers between devices  1030 us (79%)
  local copies, waits for them, and re-layouts  84 us (6%)
  blocking collectives  74.6 us (6%)
  matrix products  64.6 us (5%)
  other arithmetic  34.8 us (3%)
  between operations  14.3 us (1%)
    all_gather x1, waiting for transfers between devices, body(): lax.all_gather(own_columns, 'dp', axis=1, tiled=True)  303 us
    all_gather x1, waiting for transfers between devices, body(): lax.all_gather(values_local, 'dp', axis=0, tiled=True)  188 us
    all_gather x1, waiting for transfers between devices, body(): lax.all_gather(keys_local, 'dp', axis=0, tiled=True)  150 us
    psum x1, waiting for transfers between devices, body(): lax.psum(branch_part, 'member')  129 us
    all_gather x1, waiting for transfers between devices, body(): summed = jnp.sum(lax.all_gather(context, 'member'), axis=0)  111 us
    reduce_scatter x1, waiting for transfers between devices, body(): lax.psum_scatter(grad_up, 'dp', scatter_dimension=0, tiled=True)  75.9 us
    psum x1, blocking collectives, body(): out_grad = lax.psum(out_part, 'member').astype(jnp.bfloat16)  74.6 us
    reduce_scatter x1, waiting for transfers between devices, body(): lax.psum_scatter(grad_down, 'dp', scatter_dimension=0, tiled=True)  74 us
  transfers between devices with their start and end apart: 8, of which 7 were waited for; matrix products, arithmetic and copies ran while one was open for 5% of the time, Pallas kernels for 0%

profile of v1, /device:TPU:8, one launch (start us, length us, event | category | flops | bytes accessed | tf_op | source)
XLA Modules:
  0.0 1305.7 jit_solution(12027609167667116974)
XLA Ops:
  7.2 0.7 all-gather.10.cloned.1.call-update
  8.0 303.0 %all-gather.10.cloned.1.call-done = bf16[1,1536,4608]{1,2,0:T(8,128)(2,1)} async-done(((bf16[1,1536,288]{1,2,0:T(8,128)(2,1)}), bf16[1,1536,4608]{1,2,0:T(8,128)(2,1)}) %all-gather.10.cloned.1.call-update) | async-done | bytes 14155792 | tf_op jit(solution)/shard_map/all_gather | solution.py:22
  311.0 9.7 fusion.8
  320.7 1.2 slice_bitcast_fusion.1
  321.9 0.7 all-gather.12.cloned.1.call-update
  323.4 188.0 %all-gather.14.cloned.1.call-done = bf16[16,172,1536]{2,1,0:T(8,128)(2,1)} async-done(((bf16[1,172,1536]{2,1,0:T(8,128)(2,1)}), bf16[16,172,1536]{2,1,0:T(8,128)(2,1)}) %all-gather.14.cloned.1.call-update) | async-done | bytes 8454160 | tf_op jit(solution)/shard_map/all_gather | solution.py:31
  511.4 17.4 %copy.18 = bf16[16,172,1536]{1,0,2:T(8,128)(2,1)} copy(bf16[16,172,1536]{2,1,0:T(8,128)(2,1)} %all-gather.14.cloned.1.call-done) | data formatting | bytes 16908288 | tf_op jit(solution)/shard_map/all_gather | solution.py:31
  528.8 22.6 %reshape.151 = bf16[2752,24,64]{0,2,1:T(8,128)(2,1)} reshape(bf16[16,172,1536]{1,0,2:T(8,128)(2,1)} %copy.18) | data formatting | bytes 16908288 | tf_op jit(solution)/shard_map/reshape | solution.py:31
  551.4 150.4 %all-gather.12.cloned.1.call-done = bf16[16,172,1536]{2,1,0:T(8,128)(2,1)} async-done(((bf16[1,172,1536]{2,1,0:T(8,128)(2,1)}), bf16[16,172,1536]{2,1,0:T(8,128)(2,1)}) %all-gather.12.cloned.1.call-update) | async-done | bytes 8454160 | tf_op jit(solution)/shard_map/all_gather | solution.py:30
  701.8 17.4 %copy.17 = bf16[16,172,1536]{1,0,2:T(8,128)(2,1)} copy(bf16[16,172,1536]{2,1,0:T(8,128)(2,1)} %all-gather.12.cloned.1.call-done) | data formatting | bytes 16908288 | tf_op jit(solution)/shard_map/all_gather | solution.py:30
  719.2 22.6 %reshape.150 = bf16[2752,24,64]{0,2,1:T(8,128)(2,1)} reshape(bf16[16,172,1536]{1,0,2:T(8,128)(2,1)} %copy.17) | data formatting | bytes 16908288 | tf_op jit(solution)/shard_map/reshape | solution.py:30
  741.8 21.4 %fusion = (f32[24,172]{1,0:T(8,128)S(1)}, f32[24,172,2752]{2,1,0:T(8,128)}) fusion(pred[172,2752]{1,0:T(8,128)(4,1)S(1)} %compare_and_fusion, bf16[172,24,64]{0,2,1:T(8,128)(2,1)S(1)} %bitcast.35, bf16[2752,24,64]{0,2,1:T(8,128)(2,1)} %reshape.150), kind=kOutput, calls=%fused_computation.2 | convolution fusion | flops 1488189440 | bytes 54913408 | tf_op jit(solution)/shard_map/qhd,khd->hqk/dot_general | solution.py:37
  763.2 22.9 %fusion.1 = f32[24,172]{1,0:T(8,128)S(1)} fusion(f32[24,172,2752]{2,1,0:T(8,128)} %get-tuple-element.13, f32[24,172]{1,0:T(8,128)S(1)} %get-tuple-element.9, pred[172,2752]{1,0:T(8,128)(4,1)S(1)} %compare_and_fusion), kind=kLoop, calls=%fused_computation.3 | loop fusion | flops 56797152 | bytes 45947392 | tf_op jit(solution)/shard_map/reduce_sum | solution.py:43
  786.2 20.8 %fusion.11 = f32[172,24,64]{0,2,1:T(8,128)S(1)} fusion(bf16[2752,24,64]{0,2,1:T(8,128)(2,1)} %reshape.151, f32[24,172,2752]{2,1,0:T(8,128)} %get-tuple-element.13, f32[24,172]{1,0:T(8,128)S(1)} %get-tuple-element.9, pred[172,2752]{1,0:T(8,128)(4,1)S(1)} %compare_and_fusion, f32[172,24]{0,1:T(8,128)S(1)} %bitcast.37, f32[172,24]{0,1:T(8,128)S(1)} %get-tuple-element.8), kind=kOutput, calls=%fused_computation.12 | convolution fusion | flops 1511442432 | bytes 55474816 | tf_op jit(solution)/shard_map/hqk,khd->qhd/dot_general | solution.py:44
  807.0 1.4 copy.19
  809.0 1.4 fusion.71
  810.4 0.7 copy-done.3
  811.0 1.2 fusion.69
  812.3 0.6 fusion.56
  812.9 111.3 %all-gather.8.cloned.1.call-done = f32[16,172,1536]{2,1,0:T(8,128)} async-done(((f32[1,172,1536]{2,1,0:T(8,128)}), f32[16,172,1536]{2,1,0:T(8,128)}) %all-gather.8.cloned.1.call-update) | async-done | bytes 16908304 | tf_op jit(solution)/shard_map/all_gather | solution.py:52
  924.3 9.5 fusion.73
  933.8 0.5 copy.22
  934.5 0.7 broadcast_multiply_fusion
  935.2 128.9 %all-reduce.3.cloned.1.call-done = f32[172,1024]{1,0:T(8,128)} async-done(((f32[172,1024]{1,0:T(8,128)}), f32[172,1024]{1,0:T(8,128)}) %all-reduce.3.cloned.1.call-update) | async-done | bytes 704528 | tf_op jit(solution)/shard_map/psum | solution.py:67
  1064.1 1.5 fusion.16
  1065.6 1.2 fusion.74
  1066.7 2.3 fusion.66
  1069.1 74.6 %all-reduce.4 = bf16[172,1024]{1,0:T(8,128)(2,1)S(1)} all-reduce(f32[172,1024]{1,0:T(8,128)S(1)} %fusion.74), channel_id=1, replica_groups=mesh['member'=16,'dp'=16] {'member'}, use_global_device_ids=true, to_apply=%region_8.9 | all-reduce | flops 176128 | bytes 1056768 | tf_op jit(solution)/shard_map/psum | solution.py:78
  1143.7 2.8 fusion.37
  1146.6 2.3 fusion.30
  1149.0 75.9 %reduce-scatter.4.cloned.1.call-done = f32[64,256]{1,0:T(8,128)} async-done(((f32[1024,256]{1,0:T(8,128)}), f32[64,256]{1,0:T(8,128)}) %reduce-scatter.4.cloned.1.call-update) | async-done | bytes 65552 | tf_op jit(solution)/shard_map/reduce_scatter | solution.py:89
  1224.9 74.0 %reduce-scatter.6.cloned.1.call-done = f32[64,256]{1,0:T(8,128)} async-done(((f32[1024,256]{1,0:T(8,128)}), f32[64,256]{1,0:T(8,128)}) %reduce-scatter.6.cloned.1.call-update) | async-done | bytes 65552 | tf_op jit(solution)/shard_map/reduce_scatter | solution.py:90
  (41 shorter events, 1.8 us)
Async XLA Ops:
  7.2 303.8 %copy-start = (bf16[172,1536]{1,0:T(8,128)(2,1)S(1)}, bf16[172,1536]{1,0:T(8,128)(2,1)}, u32[]{:S(2)}) copy-start(bf16[172,1536]{1,0:T(8,128)(2,1)} %param.7) | copy-start | bytes 1585156
  7.2 303.8 %all-gather.10.cloned.1.call-start = ((), (), s32[]{:S(2)}) async-start(), calls=%async_computation.8 | async-start | bytes 15040512 | tf_op jit(solution)/shard_map/all_gather | solution.py:22
  7.9 503.5 %all-gather.14.cloned.1.call-start = ((), (), s32[]{:S(2)}) async-start(), calls=%async_computation.10 | async-start | bytes 9191424 | tf_op jit(solution)/shard_map/all_gather | solution.py:31
  321.9 379.9 %all-gather.12.cloned.1.call-start = ((), (), s32[]{:S(2)}) async-start(), calls=%async_computation.9 | async-start | bytes 9191424 | tf_op jit(solution)/shard_map/all_gather | solution.py:30
  322.6 601.6 %all-gather.8.cloned.1.call-start = ((), (), s32[]{:S(2)}) async-start(), calls=%async_computation.4 | async-start | bytes 18382848 | tf_op jit(solution)/shard_map/all_gather | solution.py:52
  786.2 22.4 %copy-start.2 = (bf16[172,1024]{1,0:T(8,128)(2,1)S(1)}, bf16[172,1024]{1,0:T(8,128)(2,1)}, u32[]{:S(2)}) copy-start(bf16[172,1024]{1,0:T(8,128)(2,1)} %param.9) | copy-start | bytes 1056772
  786.2 22.8 %copy-start.7 = (f32[1024]{0:T(1024)S(1)}, f32[1024]{0:T(1024)}, u32[]{:S(2)}) copy-start(f32[1024]{0:T(1024)} %param.10) | copy-start | bytes 12292
  786.2 24.9 %copy-start.4 = (bf16[1024,256]{1,0:T(8,128)(2,1)S(1)}, bf16[1024,256]{1,0:T(8,128)(2,1)}, u32[]{:S(2)}) copy-start(bf16[1024,256]{1,0:T(8,128)(2,1)} %param.12) | copy-start | bytes 1572868
  808.5 255.6 %all-reduce.3.cloned.1.call-start = ((), (), s32[]{:S(2)}) async-start(), calls=%async_computation.3 | async-start | bytes 1441792 | tf_op jit(solution)/shard_map/psum | solution.py:67
  808.7 3.5 copy-start.5
  809.0 3.3 copy-start.6
  810.4 0.7 copy-start.3
  812.3 336.7 %reduce-scatter.8.cloned.1.call-start = ((), (), s32[]{:S(2)}) async-start(), calls=%async_computation.7 | async-start | bytes 557056 | tf_op jit(solution)/shard_map/reduce_scatter | solution.py:91
  812.9 485.9 %copy-start.1 = (bf16[172,1536]{1,0:T(8,128)(2,1)S(1)}, bf16[172,1536]{1,0:T(8,128)(2,1)}, u32[]{:S(2)}) copy-start(bf16[172,1536]{1,0:T(8,128)(2,1)} %param.7) | copy-start | bytes 1585156
  1069.0 155.9 %reduce-scatter.4.cloned.1.call-start = ((), (), s32[]{:S(2)}) async-start(), calls=%async_computation.5 | async-start | bytes 1114112 | tf_op jit(solution)/shard_map/reduce_scatter | solution.py:89
  1146.5 152.3 %reduce-scatter.6.cloned.1.call-start = ((), (), s32[]{:S(2)}) async-start(), calls=%async_computation.6 | async-start | bytes 1114112 | tf_op jit(solution)/shard_map/reduce_scatter | solution.py:90
Sparse Core Ops, SparseCore 0:
  9.8 301.1 all-gather.9
  322.0 189.3 all-gather.13
  513.2 188.5 all-gather.11
  808.6 115.5 all-gather.7
  926.7 137.2 all-reduce.2
  1069.1 76.8 reduce-scatter.7
  1149.1 75.7 reduce-scatter.3
  1228.0 70.8 reduce-scatter.5
